TPU v7x, 32 devices: a whole 2x2x4 slice. The times are simulated.
32 devices in a mesh: section: 2 (over core), dp: 8 (over z, x), seq: 2 (over y).
Axes of the slice: x: 2, y: 2, z: 4, core: 2. Of those that a mesh axis runs over, the one named last changes fastest.
Arguments:
- tokens: bfloat16 [4, 8, 1024, 768], P(None, 'dp', 'seq'), may hold values from -6 to 6
- segments: int32 [4, 8, 1024], P(None, 'dp'), may hold values from 0 to 4, as said below
- cotangent: bfloat16 [4, 8, 1024, 768], P(None, 'dp', 'seq'), may hold values from -6 to 6
- joint_weight: bfloat16 [2, 768, 2304], P('section'), may hold values from -0.21875 to 0.21875
- joint_bias: float32 [2, 2304], P('section'), may hold values from -2 to 2
- output_weight: bfloat16 [2, 768, 768], P('section'), may hold values from -0.21875 to 0.21875
- output_bias: float32 [2, 768], P('section'), may hold values from -2 to 2
- up_weight: bfloat16 [2, 768, 3072], P('section'), may hold values from -0.21875 to 0.21875
- up_bias: float32 [2, 3072], P('section'), may hold values from -2 to 2
- down_weight: bfloat16 [2, 3072, 768], P('section'), may hold values from -0.109375 to 0.109375
- down_bias: float32 [2, 768], P('section'), may hold values from -2 to 2
- first_gain: float32 [2, 768], P('section'), may hold values from 0.25 to 1.75
- inner_gain: float32 [2, 768], P('section'), may hold values from 0.25 to 1.75
- second_gain: float32 [2, 768], P('section'), may hold values from 0.25 to 1.75
- hidden_gain: float32 [2, 3072], P('section'), may hold values from 0.25 to 1.75
Outputs:
- hiddens: bfloat16 [2, 4, 8, 1024, 768], P('section', None, 'dp', 'seq')
- input_gradients: float32 [2, 4, 8, 1024, 768], P('section', None, 'dp', 'seq')
- joint_weight_gradient: float32 [2, 768, 2304], P('section', None, ('dp', 'seq'))
- joint_bias_gradient: float32 [2, 2304], P('section', ('dp', 'seq'))
- output_weight_gradient: float32 [2, 768, 768], P('section', None, ('dp', 'seq'))
- output_bias_gradient: float32 [2, 768], P('section', ('dp', 'seq'))
- up_weight_gradient: float32 [2, 768, 3072], P('section', None, ('dp', 'seq'))
- up_bias_gradient: float32 [2, 3072], P('section', ('dp', 'seq'))
- down_weight_gradient: float32 [2, 3072, 768], P('section', None, ('dp', 'seq'))
- down_bias_gradient: float32 [2, 768], P('section', ('dp', 'seq'))
- first_gain_gradient: float32 [2, 768], P('section', ('dp', 'seq'))
- inner_gain_gradient: float32 [2, 768], P('section', ('dp', 'seq'))
- second_gain_gradient: float32 [2, 768], P('section', ('dp', 'seq'))
- hidden_gain_gradient: float32 [2, 3072], P('section', ('dp', 'seq'))
Inputs may be any that keep to these rules, and one draw needn't show every extreme that they name: `segments`: along a row the ids never fall, and the row starts with id 0.
All inputs are finite; a program needn't handle non-finite values.
Results may differ from a plain program's by a relative error of at most 0.015.
Values may be sent and summed in bfloat16 or wider, within the bound.
A program may use at most 512 MiB of HBM per device.

v0:
```python
import jax
import jax.numpy as jnp
from jax import lax
from jax.sharding import PartitionSpec as P

HEAD_DIM = 64
EPSILON = 1e-05
MASKED = -1e30


def passed_along(value, axis, by):
    devices = lax.axis_size(axis)
    pairs = [(i, i + by) for i in range(devices) if 0 <= i + by < devices]
    return lax.ppermute(value, axis, pairs)


def layer_norm(value, gain):
    centered = value - jnp.mean(value, axis=-1, keepdims=True)
    spread = jnp.mean(centered * centered, axis=-1, keepdims=True)
    return centered * lax.rsqrt(spread + EPSILON) * gain


def feed_norm(before, gain):
    return layer_norm(jax.nn.gelu(before, approximate=False), gain)


def rotate(value, cosine, sine):
    middle = value.shape[-1] // 2
    first, second = (value[..., :middle], value[..., middle:])
    return jnp.concatenate(
        [first * cosine - second * sine, second * cosine + first * sine], axis=-1
    )


def rotate_back(incoming, cosine, sine):
    middle = incoming.shape[-1] // 2
    first, second = (incoming[..., :middle], incoming[..., middle:])
    return jnp.concatenate(
        [first * cosine + second * sine, second * cosine - first * sine], axis=-1
    )


def layer_forward(state, labels, weights, part):
    (
        joint_weight,
        joint_bias,
        output_weight,
        output_bias,
        up_weight,
        up_bias,
        down_weight,
        down_bias,
        first_gain,
        inner_gain,
        second_gain,
        hidden_gain,
    ) = weights
    row_count, piece_len, model_width = state.shape
    head_count = model_width // HEAD_DIM
    shape_heads = (row_count, piece_len, head_count, HEAD_DIM)
    offset = part * piece_len
    local_labels = lax.dynamic_slice_in_dim(labels, offset, piece_len, 1)
    starts = jnp.sum((labels[:, None, :] < local_labels[:, :, None]).astype(jnp.int32), axis=-1)
    places = offset + jnp.arange(piece_len, dtype=jnp.int32)[None, :] - starts
    inverse_rate = 1.0 / 10000.0 ** (jnp.arange(HEAD_DIM // 2, dtype=jnp.float32) * 2.0 / HEAD_DIM)
    angle = places.astype(jnp.float32)[:, :, None, None] * inverse_rate
    cosine = jnp.cos(angle)
    sine = jnp.sin(angle)
    normed = layer_norm(state, first_gain).astype(jnp.bfloat16)
    joint = jnp.dot(normed, joint_weight, preferred_element_type=jnp.float32) + joint_bias
    query = rotate(joint[..., :model_width].reshape(shape_heads), cosine, sine).astype(jnp.bfloat16)
    key = rotate(
        joint[..., model_width : 2 * model_width].reshape(shape_heads), cosine, sine
    ).astype(jnp.bfloat16)
    value = joint[..., 2 * model_width :].reshape(shape_heads).astype(jnp.bfloat16)
    keys_all, values_all = (
        lax.all_gather(key, "seq", axis=1, tiled=True),
        lax.all_gather(value, "seq", axis=1, tiled=True),
    )
    match = local_labels[:, None, :, None] == labels[:, None, None, :]
    scores = jnp.einsum(
        "rqhd,rkhd->rhqk", query, keys_all, preferred_element_type=jnp.float32
    ) * HEAD_DIM ** (-0.5)
    scores = jnp.where(match, scores, MASKED)
    peak = jnp.max(scores, axis=-1, keepdims=True)
    raised = jnp.exp(scores - peak)
    total_raised = jnp.sum(raised, axis=-1, keepdims=True)
    shares = raised / total_raised
    log_total = peak + jnp.log(total_raised)
    attended = jnp.einsum(
        "rhqk,rkhd->rqhd",
        shares.astype(jnp.bfloat16),
        values_all,
        preferred_element_type=jnp.float32,
    ).reshape(row_count, piece_len, model_width)
    inner = layer_norm(attended, inner_gain).astype(jnp.bfloat16)
    mixed = state + jnp.dot(inner, output_weight, preferred_element_type=jnp.float32) + output_bias
    normed_two = layer_norm(mixed, second_gain).astype(jnp.bfloat16)
    before = jnp.dot(normed_two, up_weight, preferred_element_type=jnp.float32) + up_bias
    hidden = feed_norm(before, hidden_gain).astype(jnp.bfloat16)
    result = mixed + jnp.dot(hidden, down_weight, preferred_element_type=jnp.float32) + down_bias
    kept = (
        state,
        normed,
        query,
        keys_all,
        values_all,
        cosine,
        sine,
        match,
        shares,
        attended,
        inner,
        mixed,
        normed_two,
        before,
        hidden,
        log_total,
        labels,
    )
    return (result, kept)


def feed_backward(kept, slope_out, weights, totals):
    (
        state,
        normed,
        query,
        keys_all,
        values_all,
        cosine,
        sine,
        match,
        shares,
        attended,
        inner,
        mixed,
        normed_two,
        before,
        hidden,
        log_total,
        labels,
    ) = kept
    (
        joint_weight,
        joint_bias,
        output_weight,
        output_bias,
        up_weight,
        up_bias,
        down_weight,
        down_bias,
        first_gain,
        inner_gain,
        second_gain,
        hidden_gain,
    ) = weights
    slope_low = slope_out.astype(jnp.bfloat16)
    totals[6] = totals[6] + jnp.einsum(
        "rcf,rcd->fd", hidden, slope_low, preferred_element_type=jnp.float32
    )
    totals[7] = totals[7] + jnp.sum(slope_low.astype(jnp.float32), axis=(0, 1))
    slope_hidden = jnp.einsum(
        "rcd,fd->rcf", slope_low, down_weight, preferred_element_type=jnp.float32
    )
    unused, puller = jax.vjp(feed_norm, before, hidden_gain)
    slope_before, slope_gain = puller(slope_hidden)
    totals[11] = totals[11] + slope_gain
    before_low = slope_before.astype(jnp.bfloat16)
    totals[4] = totals[4] + jnp.einsum(
        "rcd,rcf->df", normed_two, before_low, preferred_element_type=jnp.float32
    )
    totals[5] = totals[5] + jnp.sum(before_low.astype(jnp.float32), axis=(0, 1))
    slope_normed = jnp.einsum(
        "rcf,df->rcd", before_low, up_weight, preferred_element_type=jnp.float32
    )
    unused, puller = jax.vjp(layer_norm, mixed, second_gain)
    slope_mixed, slope_gain = puller(slope_normed)
    totals[10] = totals[10] + slope_gain
    return (slope_out + slope_mixed, totals)


def attend_backward(kept, slope_mixed, weights, totals):
    (
        state,
        normed,
        query,
        keys_all,
        values_all,
        cosine,
        sine,
        match,
        shares,
        attended,
        inner,
        mixed,
        normed_two,
        before,
        hidden,
        log_total,
        labels,
    ) = kept
    (
        joint_weight,
        joint_bias,
        output_weight,
        output_bias,
        up_weight,
        up_bias,
        down_weight,
        down_bias,
        first_gain,
        inner_gain,
        second_gain,
        hidden_gain,
    ) = weights
    row_count, piece_len, model_width = state.shape
    head_count = model_width // HEAD_DIM
    scale = HEAD_DIM ** (-0.5)
    slope_low = slope_mixed.astype(jnp.bfloat16)
    totals[2] = totals[2] + jnp.einsum(
        "rcd,rce->de", inner, slope_low, preferred_element_type=jnp.float32
    )
    totals[3] = totals[3] + jnp.sum(slope_low.astype(jnp.float32), axis=(0, 1))
    slope_inner = jnp.einsum(
        "rce,de->rcd", slope_low, output_weight, preferred_element_type=jnp.float32
    )
    unused, puller = jax.vjp(layer_norm, attended, inner_gain)
    slope_attended, slope_gain = puller(slope_inner)
    totals[9] = totals[9] + slope_gain
    slope_heads = slope_attended.astype(jnp.bfloat16).reshape(
        row_count, piece_len, head_count, HEAD_DIM
    )
    slope_shares = jnp.einsum(
        "rqhd,rkhd->rhqk", slope_heads, values_all, preferred_element_type=jnp.float32
    )
    weighted = jnp.sum(shares * slope_shares, axis=-1, keepdims=True)
    slope_scores = (shares * (slope_shares - weighted)).astype(jnp.bfloat16)
    slope_query = (
        jnp.einsum("rhqk,rkhd->rqhd", slope_scores, keys_all, preferred_element_type=jnp.float32)
        * scale
    )
    shares_low = shares.astype(jnp.bfloat16)
    key_part = (
        jnp.einsum("rhqk,rqhd->krhd", slope_scores, query, preferred_element_type=jnp.float32)
        * scale
    )
    value_part = jnp.einsum(
        "rhqk,rqhd->krhd", shares_low, slope_heads, preferred_element_type=jnp.float32
    )
    summed = lax.psum_scatter(
        jnp.concatenate([key_part, value_part], axis=-1).astype(jnp.bfloat16),
        "seq",
        scatter_dimension=0,
        tiled=True,
    ).astype(jnp.float32)
    summed = jnp.transpose(summed, (1, 0, 2, 3))
    key_raw = summed[..., :HEAD_DIM]
    slope_value = summed[..., HEAD_DIM:]
    slope_key = rotate_back(key_raw, cosine, sine)
    slope_query = rotate_back(slope_query, cosine, sine)
    flat = (row_count, piece_len, model_width)
    slope_joint = jnp.concatenate(
        [slope_query.reshape(flat), slope_key.reshape(flat), slope_value.reshape(flat)], axis=-1
    ).astype(jnp.bfloat16)
    totals[0] = totals[0] + jnp.einsum(
        "rcd,rce->de", normed, slope_joint, preferred_element_type=jnp.float32
    )
    totals[1] = totals[1] + jnp.sum(slope_joint.astype(jnp.float32), axis=(0, 1))
    slope_normed = jnp.einsum(
        "rce,de->rcd", slope_joint, joint_weight, preferred_element_type=jnp.float32
    )
    unused, puller = jax.vjp(layer_norm, state, first_gain)
    slope_state, slope_gain = puller(slope_normed)
    totals[8] = totals[8] + slope_gain
    return (slope_mixed + slope_state, totals)


def lift(vector):
    return vector.reshape(1, vector.shape[0])


def shards(
    tokens,
    segments,
    cotangent,
    joint_weight,
    joint_bias,
    output_weight,
    output_bias,
    up_weight,
    up_bias,
    down_weight,
    down_bias,
    first_gain,
    inner_gain,
    second_gain,
    hidden_gain,
):
    weights = tuple(
        (
            item[0]
            for item in (
                joint_weight,
                joint_bias,
                output_weight,
                output_bias,
                up_weight,
                up_bias,
                down_weight,
                down_bias,
                first_gain,
                inner_gain,
                second_gain,
                hidden_gain,
            )
        )
    )
    micro, row_count, piece_len, model_width = tokens.shape
    leading = lax.axis_index("section") == 0
    part = lax.axis_index("seq")
    received = jnp.zeros((row_count, piece_len, model_width), jnp.bfloat16)
    saved = []
    results = []
    for moment in range(micro + 1):
        labels = jnp.where(leading, segments[min(moment, micro - 1)], segments[max(moment - 1, 0)])
        source = jnp.where(leading, tokens[min(moment, micro - 1)], received)
        state = source.astype(jnp.float32)
        result, kept = layer_forward(state, labels, weights, part)
        sent = result.astype(jnp.bfloat16)
        results.append(sent)
        saved.append((state, labels))
        if moment < micro:
            received = passed_along(sent, "section", 1)
    totals = [jnp.zeros(item.shape, jnp.float32) for item in weights]
    back_received = jnp.zeros((row_count, piece_len, model_width), jnp.bfloat16)
    back_results = []
    for moment in range(micro + 1):
        earlier = max(moment - 1, 0)
        later = min(moment + 1, micro)
        state = jnp.where(leading, saved[earlier][0], saved[later][0])
        labels = jnp.where(leading, saved[earlier][1], saved[later][1])
        kept = layer_forward(state, labels, weights, part)[1]
        if moment < micro:
            outer = cotangent[moment].astype(jnp.float32)
        else:
            outer = jnp.zeros((row_count, piece_len, model_width), jnp.float32)
        slope_out = jnp.where(leading, back_received.astype(jnp.float32), outer)
        slope_mixed, totals = feed_backward(kept, slope_out, weights, totals)
        slope_input, totals = attend_backward(kept, slope_mixed, weights, totals)
        back_results.append(slope_input)
        if moment < micro:
            back_received = passed_along(slope_input.astype(jnp.bfloat16), "section", -1)
    reduced = (
        lax.psum_scatter(totals[0], ("dp", "seq"), scatter_dimension=1, tiled=True),
        lax.psum_scatter(lift(totals[1]), ("dp", "seq"), scatter_dimension=1, tiled=True),
        lax.psum_scatter(totals[2], ("dp", "seq"), scatter_dimension=1, tiled=True),
        lax.psum_scatter(lift(totals[3]), ("dp", "seq"), scatter_dimension=1, tiled=True),
        lax.psum_scatter(totals[4], ("dp", "seq"), scatter_dimension=1, tiled=True),
        lax.psum_scatter(lift(totals[5]), ("dp", "seq"), scatter_dimension=1, tiled=True),
        lax.psum_scatter(totals[6], ("dp", "seq"), scatter_dimension=1, tiled=True),
        lax.psum_scatter(lift(totals[7]), ("dp", "seq"), scatter_dimension=1, tiled=True),
        lax.psum_scatter(lift(totals[8]), ("dp", "seq"), scatter_dimension=1, tiled=True),
        lax.psum_scatter(lift(totals[9]), ("dp", "seq"), scatter_dimension=1, tiled=True),
        lax.psum_scatter(lift(totals[10]), ("dp", "seq"), scatter_dimension=1, tiled=True),
        lax.psum_scatter(lift(totals[11]), ("dp", "seq"), scatter_dimension=1, tiled=True),
    )
    hiddens = jnp.stack(
        [jnp.where(leading, results[index], results[index + 1]) for index in range(micro)]
    )[None]
    input_gradients = jnp.stack(
        [jnp.where(leading, back_results[index + 1], back_results[index]) for index in range(micro)]
    )[None]
    return (
        hiddens,
        input_gradients,
        reduced[0][None],
        reduced[1],
        reduced[2][None],
        reduced[3],
        reduced[4][None],
        reduced[5],
        reduced[6][None],
        reduced[7],
        reduced[8],
        reduced[9],
        reduced[10],
        reduced[11],
    )


def solution(mesh):
    return jax.shard_map(
        shards,
        mesh=mesh,
        in_specs=(
            P(None, "dp", "seq", None),
            P(None, "dp", None),
            P(None, "dp", "seq", None),
            P("section", None, None),
            P("section", None),
            P("section", None, None),
            P("section", None),
            P("section", None, None),
            P("section", None),
            P("section", None, None),
            P("section", None),
            P("section", None),
            P("section", None),
            P("section", None),
            P("section", None),
        ),
        out_specs=(
            P("section", None, "dp", "seq", None),
            P("section", None, "dp", "seq", None),
            P("section", None, ("dp", "seq")),
            P("section", ("dp", "seq")),
            P("section", None, ("dp", "seq")),
            P("section", ("dp", "seq")),
            P("section", None, ("dp", "seq")),
            P("section", ("dp", "seq")),
            P("section", None, ("dp", "seq")),
            P("section", ("dp", "seq")),
            P("section", ("dp", "seq")),
            P("section", ("dp", "seq")),
            P("section", ("dp", "seq")),
            P("section", ("dp", "seq")),
        ),
        check_vma=False,
    )
```

profile of v0, /device:TPU:0, one launch (start us, length us, event | category | flops | bytes accessed | tf_op | source)
XLA Modules:
  0.0 3620.2 jit_solution(6159310209676354836)
XLA Ops:
  66.7 20.4 all-gather.23.cloned.1.call-done
  101.3 34.7 fusion.769
  232.1 34.7 fusion.773
  330.3 20.3 all-gather.31.cloned.1.call-done
  364.8 34.7 fusion.777
  463.0 20.3 all-gather.35.cloned.1.call-done
  497.6 34.7 fusion.781
  598.3 20.1 all-gather.43.cloned.1.call-done
  632.7 34.7 fusion.785
  810.1 29.2 reduce-scatter.34.cloned.1.call-done
  980.9 34.7 fusion.798
  1042.5 35.0 fusion.796
  1091.1 34.9 fusion.792
  1139.4 34.7 fusion.794
  1234.2 62.9 %fusion.737 = (f32[512]{0:T(512)}, f32[512,3072]{1,0:T(8,128)}, f32[512,3072]{1,0:T(8,128)}, f32[512]{0:T(512)S(1)}, f32[512,3072]{1,0:T(8,128)S(1)}, /*index=5*...) fusion(f32[3072]{0:T(1024)S(1)} %bitcast.1354, ...), kind=kOutput, calls=%fused_computation.1355 | convolution fusion | flops 2832726016 | bytes 81816576 | tf_op jit(solution)/shard_map/dot_general | solution.py:99
  1402.2 35.0 reduce-scatter.36.cloned.1.call-done
  1558.4 34.6 reduce-scatter.38.cloned.1.call-done
  1712.3 35.0 reduce-scatter.40.cloned.1.call-done
  1974.1 21.7 add_add_fusion.5
  2021.7 20.6 add_add_fusion.6
  2099.8 34.7 fusion.788
  2173.7 35.7 reduce-scatter.62.cloned.1.call-done
  2210.8 124.7 %reduce-scatter.54.cloned.1.call-done = f32[48,1]{1,0:T(8,128)} async-done(((f32[768,1]{1,0:T(8,128)}), f32[48,1]{1,0:T(8,128)}) %reduce-scatter.54.cloned.1.call-update) | async-done | bytes 208
  2336.8 127.2 %reduce-scatter.66.cloned.1.call-done = f32[192,1]{1,0:T(8,128)} async-done(((f32[3072,1]{1,0:T(8,128)}), f32[192,1]{1,0:T(8,128)}) %reduce-scatter.66.cloned.1.call-update) | async-done | bytes 784
  2465.6 126.7 %reduce-scatter.56.cloned.1.call-done = f32[192,1]{1,0:T(8,128)} async-done(((f32[3072,1]{1,0:T(8,128)}), f32[192,1]{1,0:T(8,128)}) %reduce-scatter.56.cloned.1.call-update) | async-done | bytes 784
  2598.6 118.8 %reduce-scatter.60.cloned.1.call-done = f32[48,1]{1,0:T(8,128)} async-done(((f32[768,1]{1,0:T(8,128)}), f32[48,1]{1,0:T(8,128)}) %reduce-scatter.60.cloned.1.call-update) | async-done | bytes 208
  2718.8 124.7 %reduce-scatter.58.cloned.1.call-done = f32[48,1]{1,0:T(8,128)} async-done(((f32[768,1]{1,0:T(8,128)}), f32[48,1]{1,0:T(8,128)}) %reduce-scatter.58.cloned.1.call-update) | async-done | bytes 208
  2844.8 126.0 %reduce-scatter.52.cloned.1.call-done = f32[144,1]{1,0:T(8,128)} async-done(((f32[2304,1]{1,0:T(8,128)}), f32[144,1]{1,0:T(8,128)}) %reduce-scatter.52.cloned.1.call-update) | async-done | bytes 592
  2972.4 130.8 %reduce-scatter.46.cloned.1.call-done = f32[768,48]{0,1:T(8,128)} async-done(((f32[768,768]{0,1:T(8,128)}), f32[768,48]{0,1:T(8,128)}) %reduce-scatter.46.cloned.1.call-update) | async-done | bytes 147472 | tf_op jit(solution)/shard_map/reduce_scatter | solution.py:357
  3103.2 177.9 %reduce-scatter.50.cloned.1.call-done = f32[3072,48]{0,1:T(8,128)} async-done(((f32[3072,768]{0,1:T(8,128)}), f32[3072,48]{0,1:T(8,128)}) %reduce-scatter.50.cloned.1.call-update) | async-done | bytes 589840 | tf_op jit(solution)/shard_map/reduce_scatter | solution.py:361
  3281.2 176.1 %reduce-scatter.48.cloned.1.call-done = f32[768,192]{0,1:T(8,128)} async-done(((f32[768,3072]{0,1:T(8,128)}), f32[768,192]{0,1:T(8,128)}) %reduce-scatter.48.cloned.1.call-update) | async-done | bytes 589840 | tf_op jit(solution)/shard_map/reduce_scatter | solution.py:359
  3457.2 156.0 %reduce-scatter.44.cloned.1.call-done = f32[768,144]{0,1:T(8,128)} async-done(((f32[768,2304]{0,1:T(8,128)}), f32[768,144]{0,1:T(8,128)}) %reduce-scatter.44.cloned.1.call-update) | async-done | bytes 442384 | tf_op jit(solution)/shard_map/reduce_scatter | solution.py:355
  (1542 shorter events, 1507.3 us)
Async XLA Ops:
  7.2 79.9 %all-gather.23.cloned.1.call-start = ((), (), s32[]{:S(2)}) async-start(), calls=%async_computation.18 | async-start | bytes 2359296 | tf_op jit(solution)/shard_map/all_gather | solution.py:77
  61.7 156.1 %all-gather.27.cloned.1.call-start = ((), (), s32[]{:S(2)}) async-start(), calls=%async_computation.20 | async-start | bytes 2359296 | tf_op jit(solution)/shard_map/all_gather | solution.py:77
  200.9 149.7 %all-gather.31.cloned.1.call-start = ((), (), s32[]{:S(2)}) async-start(), calls=%async_computation.22 | async-start | bytes 2359296 | tf_op jit(solution)/shard_map/all_gather | solution.py:77
  329.8 153.6 %all-gather.35.cloned.1.call-start = ((), (), s32[]{:S(2)}) async-start(), calls=%async_computation.24 | async-start | bytes 2359296 | tf_op jit(solution)/shard_map/all_gather | solution.py:77
  462.6 155.9 %all-gather.43.cloned.1.call-start = ((), (), s32[]{:S(2)}) async-start(), calls=%async_computation.28 | async-start | bytes 2359296 | tf_op jit(solution)/shard_map/all_gather | solution.py:77
  598.2 241.1 %reduce-scatter.34.cloned.1.call-start = ((), (), s32[]{:S(2)}) async-start(), calls=%async_computation.29 | async-start | bytes 4718592 | tf_op jit(solution)/shard_map/reduce_scatter | solution.py:251
  795.8 171.7 %all-gather.55.cloned.1.call-start = ((), (), s32[]{:S(2)}) async-start(), calls=%async_computation.37 | async-start | bytes 2359296 | tf_op jit(solution)/shard_map/all_gather | solution.py:77
  867.3 148.3 %all-gather.53.cloned.1.call-start = ((), (), s32[]{:S(2)}) async-start(), calls=%async_computation.36 | async-start | bytes 2359296 | tf_op jit(solution)/shard_map/all_gather | solution.py:78
  873.2 155.8 %all-gather.51.cloned.1.call-start = ((), (), s32[]{:S(2)}) async-start(), calls=%async_computation.34 | async-start | bytes 2359296 | tf_op jit(solution)/shard_map/all_gather | solution.py:77
  892.7 184.8 %all-gather.59.cloned.1.call-start = ((), (), s32[]{:S(2)}) async-start(), calls=%async_computation.40 | async-start | bytes 2359296 | tf_op jit(solution)/shard_map/all_gather | solution.py:77
  913.1 212.8 %all-gather.47.cloned.1.call-start = ((), (), s32[]{:S(2)}) async-start(), calls=%async_computation.31 | async-start | bytes 2359296 | tf_op jit(solution)/shard_map/all_gather | solution.py:77
  936.5 237.7 %all-gather.49.cloned.1.call-start = ((), (), s32[]{:S(2)}) async-start(), calls=%async_computation.33 | async-start | bytes 2359296 | tf_op jit(solution)/shard_map/all_gather | solution.py:78
  941.2 244.9 %all-gather.57.cloned.1.call-start = ((), (), s32[]{:S(2)}) async-start(), calls=%async_computation.39 | async-start | bytes 2359296 | tf_op jit(solution)/shard_map/all_gather | solution.py:78
  946.0 253.8 %all-gather.45.cloned.1.call-start = ((), (), s32[]{:S(2)}) async-start(), calls=%async_computation.30 | async-start | bytes 2359296 | tf_op jit(solution)/shard_map/all_gather | solution.py:78
  963.5 473.7 %reduce-scatter.36.cloned.1.call-start = ((), (), s32[]{:S(2)}) async-start(), calls=%async_computation.32 | async-start | bytes 4718592 | tf_op jit(solution)/shard_map/reduce_scatter | solution.py:251
  1392.0 201.1 %reduce-scatter.38.cloned.1.call-start = ((), (), s32[]{:S(2)}) async-start(), calls=%async_computation.35 | async-start | bytes 4718592 | tf_op jit(solution)/shard_map/reduce_scatter | solution.py:251
  1547.8 199.4 %reduce-scatter.40.cloned.1.call-start = ((), (), s32[]{:S(2)}) async-start(), calls=%async_computation.38 | async-start | bytes 4718592 | tf_op jit(solution)/shard_map/reduce_scatter | solution.py:251
  1702.1 216.9 %reduce-scatter.42.cloned.1.call-start = ((), (), s32[]{:S(2)}) async-start(), calls=%async_computation.41 | async-start | bytes 4718592 | tf_op jit(solution)/shard_map/reduce_scatter | solution.py:251
  1854.6 199.8 %all-gather.39.cloned.1.call-start = ((), (), s32[]{:S(2)}) async-start(), calls=%async_computation.26 | async-start | bytes 2359296 | tf_op jit(solution)/shard_map/all_gather | solution.py:77
  1873.3 261.3 %all-gather.37.cloned.1.call-start = ((), (), s32[]{:S(2)}) async-start(), calls=%async_computation.25 | async-start | bytes 2359296 | tf_op jit(solution)/shard_map/all_gather | solution.py:78
  1881.7 290.7 %reduce-scatter.64.cloned.1.call-start = ((), (), s32[]{:S(2)}) async-start(), calls=%async_computation.52 | async-start | bytes 417792
  1897.0 312.5 %reduce-scatter.62.cloned.1.call-start = ((), (), s32[]{:S(2)}) async-start(), calls=%async_computation.51 | async-start | bytes 417792
  1898.7 436.8 %reduce-scatter.54.cloned.1.call-start = ((), (), s32[]{:S(2)}) async-start(), calls=%async_computation.47 | async-start | bytes 417792
  1900.5 563.6 %reduce-scatter.66.cloned.1.call-start = ((), (), s32[]{:S(2)}) async-start(), calls=%async_computation.53 | async-start | bytes 1671168
  1904.3 688.0 %reduce-scatter.56.cloned.1.call-start = ((), (), s32[]{:S(2)}) async-start(), calls=%async_computation.48 | async-start | bytes 1671168
  1908.1 809.4 %reduce-scatter.60.cloned.1.call-start = ((), (), s32[]{:S(2)}) async-start(), calls=%async_computation.50 | async-start | bytes 417792
  1928.7 914.8 %reduce-scatter.58.cloned.1.call-start = ((), (), s32[]{:S(2)}) async-start(), calls=%async_computation.49 | async-start | bytes 417792
  1933.5 1037.3 %reduce-scatter.52.cloned.1.call-start = ((), (), s32[]{:S(2)}) async-start(), calls=%async_computation.46 | async-start | bytes 1253376
  1937.8 1165.4 %reduce-scatter.46.cloned.1.call-start = ((), (), s32[]{:S(2)}) async-start(), calls=%async_computation.43 | async-start | bytes 2506752 | tf_op jit(solution)/shard_map/reduce_scatter | solution.py:357
  1944.7 1336.5 %reduce-scatter.50.cloned.1.call-start = ((), (), s32[]{:S(2)}) async-start(), calls=%async_computation.45 | async-start | bytes 10027008 | tf_op jit(solution)/shard_map/reduce_scatter | solution.py:361
  1995.9 1461.3 %reduce-scatter.48.cloned.1.call-start = ((), (), s32[]{:S(2)}) async-start(), calls=%async_computation.44 | async-start | bytes 10027008 | tf_op jit(solution)/shard_map/reduce_scatter | solution.py:359
  2042.4 1570.8 %reduce-scatter.44.cloned.1.call-start = ((), (), s32[]{:S(2)}) async-start(), calls=%async_computation.42 | async-start | bytes 7520256 | tf_op jit(solution)/shard_map/reduce_scatter | solution.py:355
  (469 other events, 4583.5 us)
Sparse Core Ops, SparseCore 0:
  57.1 29.9 all-gather.22
  89.2 27.1 all-gather.20
  190.5 27.2 all-gather.26
  219.8 27.1 all-gather.24
  323.3 27.2 all-gather.30
  352.6 27.1 all-gather.28
  456.1 27.2 all-gather.34
  485.5 27.1 all-gather.32
  591.1 27.2 all-gather.42
  795.9 43.3 reduce-scatter.33
  867.4 27.1 all-gather.54
  896.2 27.1 all-gather.52
  925.0 27.2 all-gather.50
  983.0 27.1 all-gather.46
  1392.1 45.0 reduce-scatter.35
  1547.9 45.0 reduce-scatter.37
  1702.2 45.0 reduce-scatter.39
  1854.8 44.9 reduce-scatter.41
  1901.3 27.2 all-gather.38
  1930.1 27.2 all-gather.36
  1962.6 121.6 reduce-scatter.63
  2088.8 120.6 reduce-scatter.61
  2214.8 120.6 reduce-scatter.53
  2340.3 123.6 reduce-scatter.65
  2468.7 123.5 reduce-scatter.55
  2596.9 120.4 reduce-scatter.59
  2722.8 120.6 reduce-scatter.57
  2848.1 122.6 reduce-scatter.51
  2976.3 126.8 reduce-scatter.45
  3110.4 170.6 reduce-scatter.49
  3287.3 169.9 reduce-scatter.47
  3463.8 149.2 reduce-scatter.43
  (5 shorter events, 135.7 us)
where the time goes:
time: 3630 us; the launch traced here: 3620 us
  waiting for transfers between devices  1660 us (46%)
  matrix products  941 us (26%)
  other arithmetic  744 us (20%)
  local copies, waits for them, and re-layouts  233 us (6%)
    unnamed x45, waiting for transfers between devices  785 us
    sub x10, other arithmetic, layer_forward(): raised = jnp.exp(scores - peak)  347 us
    dot_general x10, matrix products, layer_forward(): jnp.dot(normed_two, up_weight, preferred_element_type=jnp.float32) + up_bias  183 us
    reduce_scatter x1, waiting for transfers between devices, shards(): lax.psum_scatter(totals[6], ('dp', 'seq'), scatter_dimension=1, tiled=True)  178 us
    reduce_scatter x1, waiting for transfers between devices, shards(): lax.psum_scatter(totals[4], ('dp', 'seq'), scatter_dimension=1, tiled=True)  176 us
    reduce_scatter x1, waiting for transfers between devices, shards(): lax.psum_scatter(totals[0], ('dp', 'seq'), scatter_dimension=1, tiled=True)  156 us
    dot_general x10, matrix products, layer_forward(): jnp.einsum('rqhd,rkhd->rhqk', query, keys_all, preferred_element_type=jnp...  139 us
    reduce_scatter x5, waiting for transfers between devices, attend_backward(): lax.psum_scatter(jnp.concatenate([key_part, value_part], axis=-1).astype(...  134 us
  transfers between devices with their start and end apart: 45, of which 24 were waited for; matrix products, arithmetic and copies ran while one was open for 27% of the time, Pallas kernels for 0%

commit v1 on v0

--- a/solution.py
+++ b/solution.py
@@ -1,3 +1,4 @@
+import functools
 import jax
 import jax.numpy as jnp
 from jax import lax
@@ -6,6 +7,34 @@
 HEAD_DIM = 64
 EPSILON = 1e-05
 MASKED = -1e30
+
+
+def supply_core(m, dim_no):
+    x_next = list(m.shape[1:])
+    x_next[dim_no] *= m.shape[0]
+    return jnp.moveaxis(m, 0, dim_no).reshape(x_next)
+
+
+def pass_digits(s0, bus_axis):
+    even, reached = (lax.axis_size(bus_axis), lax.axis_index(bus_axis))
+    seen_now, answer = (s0[None], 1)
+    while answer < even:
+        right_arr = lax.ppermute(
+            seen_now, bus_axis, list(map(lambda jj: (jj, jj ^ answer), range(even)))
+        )
+        e_now = reached & answer == 0
+        seen_now = jnp.concatenate(
+            [jnp.where(e_now, seen_now, right_arr), jnp.where(e_now, right_arr, seen_now)]
+        )
+        answer *= 2
+    return seen_now
+
+
+def _return_all_roads(work_x, arr, along_dim):
+    return supply_core(pass_digits(work_x, arr), along_dim)
+
+
+attach_stages_all = functools.partial(_return_all_roads, arr="seq", along_dim=1)
 
 
 def passed_along(value, axis, by):
@@ -74,7 +103,7 @@
     ).astype(jnp.bfloat16)
     value = joint[..., 2 * model_width :].reshape(shape_heads).astype(jnp.bfloat16)
     keys_all, values_all = (
-        lax.all_gather(key, "seq", axis=1, tiled=True),
+        attach_stages_all(key),
         lax.all_gather(value, "seq", axis=1, tiled=True),
     )
     match = local_labels[:, None, :, None] == labels[:, None, None, :]

time: 3630 us -> 3650 us (level)
  local copies, waits for them, and re-layouts: 233 us -> 301 us
  waiting for transfers between devices: 1660 us -> 1610 us
    all_gather x10 -> x0, waiting for transfers between devices: 97.7 us -> none  [layer_forward(): lax.all_gather(key, 'seq', axis=1, tiled=True)]
    ppermute x0 -> x10, waiting for transfers between devices: none -> 89.5 us  [pass_digits(): lax.ppermute(seen_now, bus_axis, list(map(lambda jj: (jj, jj ^ answer), r...]
    unnamed x45 -> x35, waiting for transfers between devices: 785 us -> 740 us
    another operation x0 -> x10, local copies, waits for them, and re-layouts: none -> 38.6 us
    unnamed x928 -> x1008, local copies, waits for them, and re-layouts: 77.6 us -> 85.4 us
  transfers between devices with their start and end apart: 45 -> 45, of which waited for: 24 -> 25; matrix products, arithmetic and copies ran while one was open for 27% -> 29% of each run, Pallas kernels for 0% -> 0%
where the time goes in v1:
time: 3650 us; the launch traced here: 3640 us
  waiting for transfers between devices  1610 us (44%)
  matrix products  943 us (26%)
  other arithmetic  734 us (20%)
  local copies, waits for them, and re-layouts  301 us (8%)
    unnamed x35, waiting for transfers between devices  740 us
    sub x10, other arithmetic, layer_forward(): raised = jnp.exp(scores - peak)  347 us
    dot_general x10, matrix products, layer_forward(): jnp.dot(normed_two, up_weight, preferred_element_type=jnp.float32) + up_bias  187 us
    reduce_scatter x1, waiting for transfers between devices, shards(): lax.psum_scatter(totals[6], ('dp', 'seq'), scatter_dimension=1, tiled=True)  177 us
    reduce_scatter x1, waiting for transfers between devices, shards(): lax.psum_scatter(totals[4], ('dp', 'seq'), scatter_dimension=1, tiled=True)  176 us
    reduce_scatter x1, waiting for transfers between devices, shards(): lax.psum_scatter(totals[0], ('dp', 'seq'), scatter_dimension=1, tiled=True)  156 us
    dot_general x10, matrix products, layer_forward(): jnp.einsum('rqhd,rkhd->rhqk', query, keys_all, preferred_element_type=jnp...  135 us
    reduce_scatter x5, waiting for transfers between devices, attend_backward(): lax.psum_scatter(jnp.concatenate([key_part, value_part], axis=-1).astype(...  131 us
  transfers between devices with their start and end apart: 45, of which 25 were waited for; matrix products, arithmetic and copies ran while one was open for 29% of the time, Pallas kernels for 0%

profile of v1, /device:TPU:0, one launch (start us, length us, event | category | flops | bytes accessed | tf_op | source)
XLA Modules:
  0.0 3638.6 jit_solution(15097150088229232831)
XLA Ops:
  104.6 34.5 fusion.759
  240.6 34.5 fusion.763
  288.9 18.8 fusion.766
  379.4 34.5 fusion.767
  428.0 18.6 fusion.770
  516.5 34.5 fusion.771
  564.8 18.6 fusion.774
  656.5 34.5 fusion.775
  706.5 20.3 fusion.747
  838.9 27.4 reduce-scatter.34.cloned.1.call-done
  1026.0 35.0 fusion.788
  1074.4 35.0 fusion.786
  1122.8 34.7 fusion.782
  1171.0 34.8 fusion.784
  1282.3 62.9 %fusion.727 = (f32[512]{0:T(512)}, f32[512,3072]{1,0:T(8,128)}, f32[512,3072]{1,0:T(8,128)}, f32[512]{0:T(512)S(1)}, f32[512,3072]{1,0:T(8,128)S(1)}, /*index=5*...) fusion(f32[3072]{0:T(1024)S(1)} %bitcast.1385, ...), kind=kOutput, calls=%fused_computation.1385 | convolution fusion | flops 2832726016 | bytes 81816576 | tf_op jit(solution)/shard_map/dot_general | solution.py:128
  1448.1 33.6 reduce-scatter.36.cloned.1.call-done
  1604.0 34.8 reduce-scatter.38.cloned.1.call-done
  1759.0 35.0 reduce-scatter.40.cloned.1.call-done
  2006.2 21.7 add_add_fusion.5
  2053.8 20.7 add_add_fusion.6
  2162.0 34.7 fusion.778
  2210.7 18.7 fusion.781
  2238.0 116.1 %reduce-scatter.54.cloned.1.call-done = f32[48,1]{1,0:T(8,128)} async-done(((f32[768,1]{1,0:T(8,128)}), f32[48,1]{1,0:T(8,128)}) %reduce-scatter.54.cloned.1.call-update) | async-done | bytes 208
  2355.4 127.2 %reduce-scatter.66.cloned.1.call-done = f32[192,1]{1,0:T(8,128)} async-done(((f32[3072,1]{1,0:T(8,128)}), f32[192,1]{1,0:T(8,128)}) %reduce-scatter.66.cloned.1.call-update) | async-done | bytes 784
  2484.2 126.6 %reduce-scatter.56.cloned.1.call-done = f32[192,1]{1,0:T(8,128)} async-done(((f32[3072,1]{1,0:T(8,128)}), f32[192,1]{1,0:T(8,128)}) %reduce-scatter.56.cloned.1.call-update) | async-done | bytes 784
  2617.1 118.9 %reduce-scatter.60.cloned.1.call-done = f32[48,1]{1,0:T(8,128)} async-done(((f32[768,1]{1,0:T(8,128)}), f32[48,1]{1,0:T(8,128)}) %reduce-scatter.60.cloned.1.call-update) | async-done | bytes 208
  2737.3 124.7 %reduce-scatter.58.cloned.1.call-done = f32[48,1]{1,0:T(8,128)} async-done(((f32[768,1]{1,0:T(8,128)}), f32[48,1]{1,0:T(8,128)}) %reduce-scatter.58.cloned.1.call-update) | async-done | bytes 208
  2863.3 126.3 %reduce-scatter.52.cloned.1.call-done = f32[144,1]{1,0:T(8,128)} async-done(((f32[2304,1]{1,0:T(8,128)}), f32[144,1]{1,0:T(8,128)}) %reduce-scatter.52.cloned.1.call-update) | async-done | bytes 592
  2991.1 130.7 %reduce-scatter.46.cloned.1.call-done = f32[768,48]{0,1:T(8,128)} async-done(((f32[768,768]{0,1:T(8,128)}), f32[768,48]{0,1:T(8,128)}) %reduce-scatter.46.cloned.1.call-update) | async-done | bytes 147472 | tf_op jit(solution)/shard_map/reduce_scatter | solution.py:386
  3121.8 177.4 %reduce-scatter.50.cloned.1.call-done = f32[3072,48]{0,1:T(8,128)} async-done(((f32[3072,768]{0,1:T(8,128)}), f32[3072,48]{0,1:T(8,128)}) %reduce-scatter.50.cloned.1.call-update) | async-done | bytes 589840 | tf_op jit(solution)/shard_map/reduce_scatter | solution.py:390
  3299.3 176.0 %reduce-scatter.48.cloned.1.call-done = f32[768,192]{0,1:T(8,128)} async-done(((f32[768,3072]{0,1:T(8,128)}), f32[768,192]{0,1:T(8,128)}) %reduce-scatter.48.cloned.1.call-update) | async-done | bytes 589840 | tf_op jit(solution)/shard_map/reduce_scatter | solution.py:388
  3475.3 156.0 %reduce-scatter.44.cloned.1.call-done = f32[768,144]{0,1:T(8,128)} async-done(((f32[768,2304]{0,1:T(8,128)}), f32[768,144]{0,1:T(8,128)}) %reduce-scatter.44.cloned.1.call-update) | async-done | bytes 442384 | tf_op jit(solution)/shard_map/reduce_scatter | solution.py:384
  (1648 shorter events, 1560.4 us)
Async XLA Ops:
  7.2 131.9 %all-gather.11.cloned.1.call-start = ((), (), s32[]{:S(2)}) async-start(), calls=%async_computation.17 | async-start | bytes 2359296 | tf_op jit(solution)/shard_map/all_gather | solution.py:107
  65.4 209.6 %all-gather.13.cloned.1.call-start = ((), (), s32[]{:S(2)}) async-start(), calls=%async_computation.18 | async-start | bytes 2359296 | tf_op jit(solution)/shard_map/all_gather | solution.py:107
  207.8 206.1 %all-gather.15.cloned.1.call-start = ((), (), s32[]{:S(2)}) async-start(), calls=%async_computation.19 | async-start | bytes 2359296 | tf_op jit(solution)/shard_map/all_gather | solution.py:107
  340.0 211.0 %all-gather.17.cloned.1.call-start = ((), (), s32[]{:S(2)}) async-start(), calls=%async_computation.20 | async-start | bytes 2359296 | tf_op jit(solution)/shard_map/all_gather | solution.py:107
  480.5 210.4 %all-gather.21.cloned.1.call-start = ((), (), s32[]{:S(2)}) async-start(), calls=%async_computation.22 | async-start | bytes 2359296 | tf_op jit(solution)/shard_map/all_gather | solution.py:107
  619.8 246.5 %reduce-scatter.34.cloned.1.call-start = ((), (), s32[]{:S(2)}) async-start(), calls=%async_computation.23 | async-start | bytes 4718592 | tf_op jit(solution)/shard_map/reduce_scatter | solution.py:280
  819.0 390.3 %all-gather.27.cloned.1.call-start = ((), (), s32[]{:S(2)}) async-start(), calls=%async_computation.28 | async-start | bytes 2359296 | tf_op jit(solution)/shard_map/all_gather | solution.py:107
  887.2 318.6 %collective-permute-start.10 = (bf16[1,512,768]{2,1,0:T(8,128)(2,1)}, bf16[1,512,768]{2,1,0:T(8,128)(2,1)}, u32[]{:S(2)}, u32[]{:S(2)}) collective-permute-start(bf16[1,512,768]{2,1,0:T(8,128)(2,1)} %fusion.715), channel_id=1, source_target_pairs={{16,0},{17,1},{18,2},{19,3},{20,4},{21,5},{22,6},{23,7},{24,8},{25... | collective-permute-start | bytes 2359304 | tf_op jit(solution)/shard_map/ppermute | solution.py:43
  899.6 67.4 %collective-permute-start.15 = (bf16[1,1,512,12,64]{2,4,3,1,0:T(8,128)(2,1)}, bf16[1,1,512,12,64]{2,4,3,1,0:T(8,128)(2,1)}, u32[]{:S(2)}, u32[]{:S(2)}) collective-permute-start(bf16[1,1,512,12,64]{2,4,3,1,0:T(8,128)(2,1)} %pad_maximum_fusion.42), channel_id=1, source_target_pairs={{0,1},{1,0},{2,3},{3,2},{4,5},{5,4},{6,7},{7,6},{8,9},{9,8},{10,11... | collective-permute-start | bytes 2359304 | tf_op jit(solution)/shard_map/ppermute | solution.py:22
  902.2 319.0 %all-gather.25.cloned.1.call-start = ((), (), s32[]{:S(2)}) async-start(), calls=%async_computation.26 | async-start | bytes 2359296 | tf_op jit(solution)/shard_map/all_gather | solution.py:107
  920.7 54.8 %collective-permute-start.13 = (bf16[1,1,512,12,64]{2,4,3,1,0:T(8,128)(2,1)}, bf16[1,1,512,12,64]{2,4,3,1,0:T(8,128)(2,1)}, u32[]{:S(2)}, u32[]{:S(2)}) collective-permute-start(bf16[1,1,512,12,64]{2,4,3,1,0:T(8,128)(2,1)} %pad_maximum_fusion.40), channel_id=1, source_target_pairs={{0,1},{1,0},{2,3},{3,2},{4,5},{5,4},{6,7},{7,6},{8,9},{9,8},{10,11... | collective-permute-start | bytes 2359304 | tf_op jit(solution)/shard_map/ppermute | solution.py:22
  924.7 308.6 %all-gather.29.cloned.1.call-start = ((), (), s32[]{:S(2)}) async-start(), calls=%async_computation.30 | async-start | bytes 2359296 | tf_op jit(solution)/shard_map/all_gather | solution.py:107
  942.3 41.6 %collective-permute-start.17 = (bf16[1,1,512,12,64]{2,4,3,1,0:T(8,128)(2,1)}, bf16[1,1,512,12,64]{2,4,3,1,0:T(8,128)(2,1)}, u32[]{:S(2)}, u32[]{:S(2)}) collective-permute-start(bf16[1,1,512,12,64]{2,4,3,1,0:T(8,128)(2,1)} %pad_maximum_fusion.44), channel_id=1, source_target_pairs={{0,1},{1,0},{2,3},{3,2},{4,5},{5,4},{6,7},{7,6},{8,9},{9,8},{10,11... | collective-permute-start | bytes 2359304 | tf_op jit(solution)/shard_map/ppermute | solution.py:22
  945.1 301.9 %all-gather.23.cloned.1.call-start = ((), (), s32[]{:S(2)}) async-start(), calls=%async_computation.24 | async-start | bytes 2359296 | tf_op jit(solution)/shard_map/all_gather | solution.py:107
  962.9 41.0 %collective-permute-start.11 = (bf16[1,1,512,12,64]{2,4,3,1,0:T(8,128)(2,1)}, bf16[1,1,512,12,64]{2,4,3,1,0:T(8,128)(2,1)}, u32[]{:S(2)}, u32[]{:S(2)}) collective-permute-start(bf16[1,1,512,12,64]{2,4,3,1,0:T(8,128)(2,1)} %pad_maximum_fusion.38), channel_id=1, source_target_pairs={{0,1},{1,0},{2,3},{3,2},{4,5},{5,4},{6,7},{7,6},{8,9},{9,8},{10,11... | collective-permute-start | bytes 2359304 | tf_op jit(solution)/shard_map/ppermute | solution.py:22
  966.9 514.8 %reduce-scatter.36.cloned.1.call-start = ((), (), s32[]{:S(2)}) async-start(), calls=%async_computation.25 | async-start | bytes 4718592 | tf_op jit(solution)/shard_map/reduce_scatter | solution.py:280
  1437.9 200.8 %reduce-scatter.38.cloned.1.call-start = ((), (), s32[]{:S(2)}) async-start(), calls=%async_computation.27 | async-start | bytes 4718592 | tf_op jit(solution)/shard_map/reduce_scatter | solution.py:280
  1593.5 200.5 %reduce-scatter.40.cloned.1.call-start = ((), (), s32[]{:S(2)}) async-start(), calls=%async_computation.29 | async-start | bytes 4718592 | tf_op jit(solution)/shard_map/reduce_scatter | solution.py:280
  1748.8 202.3 %reduce-scatter.42.cloned.1.call-start = ((), (), s32[]{:S(2)}) async-start(), calls=%async_computation.31 | async-start | bytes 4718592 | tf_op jit(solution)/shard_map/reduce_scatter | solution.py:280
  1902.4 294.3 %all-gather.19.cloned.1.call-start = ((), (), s32[]{:S(2)}) async-start(), calls=%async_computation.21 | async-start | bytes 2359296 | tf_op jit(solution)/shard_map/all_gather | solution.py:107
  1914.1 321.3 %reduce-scatter.64.cloned.1.call-start = ((), (), s32[]{:S(2)}) async-start(), calls=%async_computation.42 | async-start | bytes 417792
  1939.8 296.9 %reduce-scatter.62.cloned.1.call-start = ((), (), s32[]{:S(2)}) async-start(), calls=%async_computation.41 | async-start | bytes 417792
  1941.5 412.6 %reduce-scatter.54.cloned.1.call-start = ((), (), s32[]{:S(2)}) async-start(), calls=%async_computation.37 | async-start | bytes 417792
  1943.2 539.4 %reduce-scatter.66.cloned.1.call-start = ((), (), s32[]{:S(2)}) async-start(), calls=%async_computation.43 | async-start | bytes 1671168
  1947.0 663.7 %reduce-scatter.56.cloned.1.call-start = ((), (), s32[]{:S(2)}) async-start(), calls=%async_computation.38 | async-start | bytes 1671168
  1950.8 785.2 %reduce-scatter.60.cloned.1.call-start = ((), (), s32[]{:S(2)}) async-start(), calls=%async_computation.40 | async-start | bytes 417792
  1960.6 901.4 %reduce-scatter.58.cloned.1.call-start = ((), (), s32[]{:S(2)}) async-start(), calls=%async_computation.39 | async-start | bytes 417792
  1965.5 1024.1 %reduce-scatter.52.cloned.1.call-start = ((), (), s32[]{:S(2)}) async-start(), calls=%async_computation.36 | async-start | bytes 1253376
  1969.7 1152.1 %reduce-scatter.46.cloned.1.call-start = ((), (), s32[]{:S(2)}) async-start(), calls=%async_computation.33 | async-start | bytes 2506752 | tf_op jit(solution)/shard_map/reduce_scatter | solution.py:386
  1976.4 1322.9 %reduce-scatter.50.cloned.1.call-start = ((), (), s32[]{:S(2)}) async-start(), calls=%async_computation.35 | async-start | bytes 10027008 | tf_op jit(solution)/shard_map/reduce_scatter | solution.py:390
  2027.9 1447.3 %reduce-scatter.48.cloned.1.call-start = ((), (), s32[]{:S(2)}) async-start(), calls=%async_computation.34 | async-start | bytes 10027008 | tf_op jit(solution)/shard_map/reduce_scatter | solution.py:388
  2074.5 1556.8 %reduce-scatter.44.cloned.1.call-start = ((), (), s32[]{:S(2)}) async-start(), calls=%async_computation.32 | async-start | bytes 7520256 | tf_op jit(solution)/shard_map/reduce_scatter | solution.py:384
  (509 other events, 4058.4 us)
Sparse Core Ops, SparseCore 0:
  65.5 29.9 all-gather.10
  207.9 27.5 all-gather.12
  340.1 30.4 all-gather.14
  480.7 28.8 all-gather.16
  619.9 29.3 all-gather.20
  819.1 47.1 reduce-scatter.33
  902.4 46.2 all-gather.26
  950.3 44.1 all-gather.24
  996.1 27.1 all-gather.28
  1024.8 27.1 all-gather.22
  1438.0 43.6 reduce-scatter.35
  1593.7 45.0 reduce-scatter.37
  1749.0 45.0 reduce-scatter.39
  1902.5 44.9 reduce-scatter.41
  1949.0 27.1 all-gather.18
  1981.5 121.5 reduce-scatter.63
  2107.6 120.6 reduce-scatter.61
  2233.5 120.5 reduce-scatter.53
  2358.9 123.6 reduce-scatter.65
  2487.3 123.4 reduce-scatter.55
  2615.4 120.5 reduce-scatter.59
  2741.3 120.6 reduce-scatter.57
  2866.8 122.7 reduce-scatter.51
  2994.9 126.8 reduce-scatter.45
  3129.0 170.1 reduce-scatter.49
  3305.4 169.8 reduce-scatter.47
  3481.9 149.3 reduce-scatter.43
